TPU v7x, 128 devices: a whole 4x4x4 slice. The times are simulated.
128 devices in a mesh: wide: 16 (over y, x), narrow: 8 (over z, core).
Axes of the slice: x: 4, y: 4, z: 4, core: 2. Of those that a mesh axis runs over, the one named last changes fastest.
Arguments:
- tokens: bfloat16 [256, 128, 1536], P('wide'), may hold values from -8 to 8
- ln_gain: bfloat16 [1536], replicated, may hold values from 0.3984375 to 1.59375
- gate_weight: bfloat16 [1536, 8960], P(None, 'narrow'), may hold values from -0.15625 to 0.15625
- up_weight: bfloat16 [1536, 8960], P(None, 'narrow'), may hold values from -0.15625 to 0.15625
- down_weight: bfloat16 [8960, 1536], P('narrow'), may hold values from -0.0625 to 0.0625
- out_gain: bfloat16 [1536], replicated, may hold values from 0.25 to 1.75
- shard_ids: int32 [256], P('wide'), may hold values from 0 to 15, as said below
- slab_old: bfloat16 [262144, 1536], P(('wide', 'narrow')), may hold values from -8 to 8
- queries: bfloat16 [16, 64, 1536], P('wide'), may hold values from -12 to 12
- positives: int32 [16, 64], P('wide'), may hold values from 0 to 262399
- owners: int32 [4], replicated, may hold values from 0 to 15
Outputs:
- index_new: bfloat16 [16, 16, 2, 1536], P('wide', 'narrow')
- losses: float32 [4, 64], replicated
Inputs may be any that keep to these rules, and one draw needn't show every extreme that they name: `shard_ids`: among the 16 passages of one index of wide at most 2 have the same shard id; in every draw one shard id is held by exactly 2 passages of every index of wide.
All inputs are finite; a program needn't handle non-finite values.
Results may differ from a plain program's by a relative error of at most 0.0029.
Values may be sent and summed in bfloat16 or wider, within the bound.
No kernel may reach another device: no remote copies, remote signals or barrier semaphores. Data moves between devices by JAX's collectives and lax.ppermute only.
A program may use at most 128 MiB of HBM per device.

v0:
```python
import math
import jax
import jax.numpy as jnp
from jax import lax
from jax.sharding import PartitionSpec as P

EPS = 1e-06


def spread(x, axis, root):
    mine = lax.axis_index(axis) == root
    return lax.psum(jnp.where(mine, x, jnp.zeros_like(x)), axis)


def rms_scale(values):
    return lax.rsqrt(jnp.mean(values * values, axis=-1, keepdims=True) + EPS)


def local(
    tokens,
    ln_gain,
    gate_weight,
    up_weight,
    down_weight,
    out_gain,
    shard_ids,
    slab_old,
    queries,
    positives,
    owners,
):
    passages, seq_len, width = tokens.shape
    narrow_count = lax.axis_size("narrow")
    wide_count = lax.axis_size("wide")
    narrow_rank = lax.axis_index("narrow")
    wide_rank = lax.axis_index("wide")
    piece_width = width // narrow_count
    capacity = 2 * passages // wide_count
    values = tokens.astype(jnp.float32)
    normed = (values * rms_scale(values) * ln_gain.astype(jnp.float32)).astype(jnp.bfloat16)
    normed = normed.reshape(passages * seq_len, width)
    gate = jnp.dot(normed, gate_weight, preferred_element_type=jnp.float32)
    upward = jnp.dot(normed, up_weight, preferred_element_type=jnp.float32)
    hidden = (jax.nn.silu(gate) * upward).astype(jnp.bfloat16)
    partial_value = jnp.dot(hidden, down_weight, preferred_element_type=jnp.float32)
    pooled_part = jnp.mean(partial_value.reshape(passages, seq_len, width), axis=1)
    token_mean = jnp.mean(values, axis=1)
    offset = narrow_rank * piece_width
    pooled = lax.psum(pooled_part, "narrow") + token_mean
    norm_scale = rms_scale(pooled)
    own_piece = lax.dynamic_slice_in_dim(pooled, offset, piece_width, 1)
    gain_piece = lax.dynamic_slice_in_dim(out_gain.astype(jnp.float32), offset, piece_width, 0)
    embedding = (own_piece * norm_scale * gain_piece).astype(jnp.bfloat16)
    positions = jnp.arange(passages, dtype=jnp.int32)
    earlier = positions[:, None] > positions[None, :]
    same = shard_ids[:, None] == shard_ids[None, :]
    rank = jnp.sum((earlier & same).astype(jnp.int32), axis=1)
    slots = shard_ids * capacity + rank
    dispatch = slots[None, :] == jnp.arange(wide_count * capacity, dtype=jnp.int32)[:, None]
    outgoing = jnp.dot(dispatch.astype(jnp.bfloat16), embedding, preferred_element_type=jnp.float32)
    outgoing = outgoing.astype(jnp.bfloat16).reshape(wide_count, capacity, piece_width)
    numbers = wide_rank * passages + positions
    slot_numbers = jnp.sum(jnp.where(dispatch, numbers[None, :] + 1, 0), axis=1) - 1
    slot_numbers = slot_numbers.reshape(wide_count, capacity, 1)
    arrived, arrived_numbers = (
        lax.all_to_all(
            lax.all_to_all(outgoing, "wide", split_axis=0, concat_axis=0, tiled=True),
            "narrow",
            split_axis=0,
            concat_axis=2,
            tiled=True,
        ),
        lax.all_to_all(
            lax.all_to_all(slot_numbers, "wide", split_axis=0, concat_axis=0, tiled=True),
            "narrow",
            split_axis=0,
            concat_axis=2,
            tiled=True,
        ),
    )
    old_total = slab_old.shape[0] * wide_count * narrow_count
    new_rows = arrived.reshape(-1, width)
    new_numbers = arrived_numbers[:, :, 0].reshape(-1)
    valid = (new_numbers >= 0)[None, :]
    new_global = old_total + new_numbers
    device_linear = wide_rank * narrow_count + narrow_rank
    old_global = device_linear * slab_old.shape[0] + jnp.arange(slab_old.shape[0], dtype=jnp.int32)
    scale = 1.0 / math.sqrt(width)
    contract = (((1,), (1,)), ((), ()))
    block_size = queries.shape[1]
    step_count = owners.shape[0]

    def score_rows(block, positive):
        old_scores = (
            lax.dot_general(block, slab_old, contract, preferred_element_type=jnp.float32) * scale
        )
        new_scores = (
            lax.dot_general(block, new_rows, contract, preferred_element_type=jnp.float32) * scale
        )
        masked = jnp.where(valid, new_scores, -jnp.inf)
        local_max = jnp.maximum(jnp.max(old_scores, axis=1), jnp.max(masked, axis=1))
        hit_old = old_global[None, :] == positive[:, None]
        hit_new = valid & (new_global[None, :] == positive[:, None])
        local_positive = jnp.sum(jnp.where(hit_old, old_scores, 0.0), axis=1) + jnp.sum(
            jnp.where(hit_new, new_scores, 0.0), axis=1
        )
        largest = lax.pmax(local_max, ("wide", "narrow"))
        local_total = jnp.sum(jnp.exp(old_scores - largest[:, None]), axis=1)
        local_total = local_total + jnp.sum(
            jnp.where(valid, jnp.exp(new_scores - largest[:, None]), 0.0), axis=1
        )
        total, picked = lax.psum((local_total, local_positive), ("wide", "narrow"))
        return largest + jnp.log(total) - picked

    def step_body(step, losses):
        owner = owners[step]
        block, positive = (spread(queries[0], "wide", owner), spread(positives[0], "wide", owner))
        loss = score_rows(block, positive)
        return lax.dynamic_update_slice_in_dim(losses, loss[None, :], step, 0)

    start_losses = jnp.zeros((step_count, block_size), jnp.float32)
    losses = lax.fori_loop(0, step_count, step_body, start_losses)
    return (arrived[None], losses)


def solution(mesh):
    return jax.shard_map(
        local,
        mesh=mesh,
        in_specs=(
            P("wide", None, None),
            P(),
            P(None, "narrow"),
            P(None, "narrow"),
            P("narrow", None),
            P(),
            P("wide"),
            P(("wide", "narrow"), None),
            P("wide", None, None),
            P("wide", None),
            P(),
        ),
        out_specs=(P("wide", "narrow", None, None), P()),
        check_vma=False,
    )
```

profile of v0, /device:TPU:1, one launch (start us, length us, event | category | flops | bytes accessed | tf_op | source)
XLA Modules:
  0.0 1026.5 jit_solution(8330299875181176620)
XLA Ops:
  17.2 9.7 fusion.16
  26.9 22.3 %bitcast_reduce_fusion = f32[16,1536]{1,0:T(8,128)} fusion(bf16[1120,1536]{1,0:T(8,128)(2,1)} %param.17, bf16[2048,1536]{1,0:T(8,128)(2,1)} %bitcast.51, bf16[1536,1120]{0,1:T(8,128)(2,1)} %param.16, f32[2048,1120]{0,1:T(8,128)} %fusion.16), kind=kOutput, calls=%fused_computation.19 | convolution fusion | flops 14109745152 | bytes 22446080 | tf_op jit(solution)/shard_map/dot_general | solution.py:45
  51.8 7.6 all-to-all-start.2
  65.7 7.6 all-to-all-start.3
  78.1 32.4 %all-reduce.6.cloned.1.call-done = f32[16,1536]{1,0:T(8,128)} async-done(((f32[16,1536]{1,0:T(8,128)}), f32[16,1536]{1,0:T(8,128)}) %all-reduce.6.cloned.1.call-update) | async-done | bytes 98320 | tf_op jit(solution)/shard_map/psum | solution.py:49
  113.1 6.6 all-to-all-start
  126.2 7.2 all-to-all-start.1
  138.8 881.1 %while.14 = (s32[]{:T(128)}, f32[4,64]{1,0:T(4,128)}, s32[4]{0:T(128)}, bf16[1,64,1536]{2,1,0:T(8,128)(2,1)}, bf16[2048,1536]{1,0:T(8,128)(2,1)}, /*index=5*/pre...) while((s32[]{:T(128)}, f32[4,64]{1,0:T(4,128)}, ...), condition=%wide.region_19.20_spmd.clone, body=%wide.region_7.19_spmd.clone.sunk | while | flops 404558592 | bytes 10132520 | solution.py:122
  141.6 9.3 psum.59
  150.9 69.7 %all-reduce.8.cloned.1.call-done = bf16[64,1536]{1,0:T(8,128)(2,1)} async-done(((bf16[64,1536]{1,0:T(8,128)(2,1)}), bf16[64,1536]{1,0:T(8,128)(2,1)}) %all-reduce.8.cloned.1.call-update) | async-done | bytes 196624 | tf_op jit(solution)/shard_map/while/body/eval_jaxpr/psum | solution.py:12
  226.6 66.3 %pmax.13 = f32[64]{0:T(128)S(1)} all-reduce(f32[64]{0:T(128)S(1)} %max.11), channel_id=1, replica_groups=mesh['wide'=16,'narrow'=8] {'wide','narrow'}, use_global_device_ids=true, to_apply=%region_11.11 | all-reduce | flops 64 | bytes 512 | tf_op jit(solution)/shard_map/while/body/eval_jaxpr/pmax | solution.py:107
  294.4 62.5 %all-reduce.2 = (f32[64]{0:T(128)S(1)}, f32[64]{0:T(128)S(1)}) all-reduce(f32[64]{0:T(128)S(1)} %add.187, f32[64]{0:T(128)S(1)} %add.188), channel_id=1, replica_groups=mesh['wide'=16,'narrow'=8] {'wide','narrow'}, use_global_device_ids=true, to_apply=%region_18.18 | all-reduce | flops 128 | bytes 1024 | tf_op jit(solution)/shard_map/while/body/eval_jaxpr/psum | solution.py:112
  361.0 10.9 %psum.59 = s32[64]{0:T(128)S(1)} all-reduce(s32[64]{0:T(128)S(1)} %fusion.37), channel_id=1, replica_groups=mesh['wide'=16,'narrow'=8] {'wide'}, use_global_device_ids=true, to_apply=%region_15.15 | all-reduce | flops 64 | bytes 512 | tf_op jit(solution)/shard_map/while/body/eval_jaxpr/psum | solution.py:12
  371.8 69.6 %all-reduce.8.cloned.1.call-done = bf16[64,1536]{1,0:T(8,128)(2,1)} async-done(((bf16[64,1536]{1,0:T(8,128)(2,1)}), bf16[64,1536]{1,0:T(8,128)(2,1)}) %all-reduce.8.cloned.1.call-update) | async-done | bytes 196624 | tf_op jit(solution)/shard_map/while/body/eval_jaxpr/psum | solution.py:12
  447.4 66.4 %pmax.13 = f32[64]{0:T(128)S(1)} all-reduce(f32[64]{0:T(128)S(1)} %max.11), channel_id=1, replica_groups=mesh['wide'=16,'narrow'=8] {'wide','narrow'}, use_global_device_ids=true, to_apply=%region_11.11 | all-reduce | flops 64 | bytes 512 | tf_op jit(solution)/shard_map/while/body/eval_jaxpr/pmax | solution.py:107
  515.2 62.5 %all-reduce.2 = (f32[64]{0:T(128)S(1)}, f32[64]{0:T(128)S(1)}) all-reduce(f32[64]{0:T(128)S(1)} %add.187, f32[64]{0:T(128)S(1)} %add.188), channel_id=1, replica_groups=mesh['wide'=16,'narrow'=8] {'wide','narrow'}, use_global_device_ids=true, to_apply=%region_18.18 | all-reduce | flops 128 | bytes 1024 | tf_op jit(solution)/shard_map/while/body/eval_jaxpr/psum | solution.py:112
  583.3 9.0 psum.59
  592.3 69.5 %all-reduce.8.cloned.1.call-done = bf16[64,1536]{1,0:T(8,128)(2,1)} async-done(((bf16[64,1536]{1,0:T(8,128)(2,1)}), bf16[64,1536]{1,0:T(8,128)(2,1)}) %all-reduce.8.cloned.1.call-update) | async-done | bytes 196624 | tf_op jit(solution)/shard_map/while/body/eval_jaxpr/psum | solution.py:12
  667.9 66.3 %pmax.13 = f32[64]{0:T(128)S(1)} all-reduce(f32[64]{0:T(128)S(1)} %max.11), channel_id=1, replica_groups=mesh['wide'=16,'narrow'=8] {'wide','narrow'}, use_global_device_ids=true, to_apply=%region_11.11 | all-reduce | flops 64 | bytes 512 | tf_op jit(solution)/shard_map/while/body/eval_jaxpr/pmax | solution.py:107
  735.7 62.5 %all-reduce.2 = (f32[64]{0:T(128)S(1)}, f32[64]{0:T(128)S(1)}) all-reduce(f32[64]{0:T(128)S(1)} %add.187, f32[64]{0:T(128)S(1)} %add.188), channel_id=1, replica_groups=mesh['wide'=16,'narrow'=8] {'wide','narrow'}, use_global_device_ids=true, to_apply=%region_18.18 | all-reduce | flops 128 | bytes 1024 | tf_op jit(solution)/shard_map/while/body/eval_jaxpr/psum | solution.py:112
  802.2 11.2 %psum.59 = s32[64]{0:T(128)S(1)} all-reduce(s32[64]{0:T(128)S(1)} %fusion.37), channel_id=1, replica_groups=mesh['wide'=16,'narrow'=8] {'wide'}, use_global_device_ids=true, to_apply=%region_15.15 | all-reduce | flops 64 | bytes 512 | tf_op jit(solution)/shard_map/while/body/eval_jaxpr/psum | solution.py:12
  813.4 68.9 %all-reduce.8.cloned.1.call-done = bf16[64,1536]{1,0:T(8,128)(2,1)} async-done(((bf16[64,1536]{1,0:T(8,128)(2,1)}), bf16[64,1536]{1,0:T(8,128)(2,1)}) %all-reduce.8.cloned.1.call-update) | async-done | bytes 196624 | tf_op jit(solution)/shard_map/while/body/eval_jaxpr/psum | solution.py:12
  888.4 66.3 %pmax.13 = f32[64]{0:T(128)S(1)} all-reduce(f32[64]{0:T(128)S(1)} %max.11), channel_id=1, replica_groups=mesh['wide'=16,'narrow'=8] {'wide','narrow'}, use_global_device_ids=true, to_apply=%region_11.11 | all-reduce | flops 64 | bytes 512 | tf_op jit(solution)/shard_map/while/body/eval_jaxpr/pmax | solution.py:107
  956.2 62.5 %all-reduce.2 = (f32[64]{0:T(128)S(1)}, f32[64]{0:T(128)S(1)}) all-reduce(f32[64]{0:T(128)S(1)} %add.187, f32[64]{0:T(128)S(1)} %add.188), channel_id=1, replica_groups=mesh['wide'=16,'narrow'=8] {'wide','narrow'}, use_global_device_ids=true, to_apply=%region_18.18 | all-reduce | flops 128 | bytes 1024 | tf_op jit(solution)/shard_map/while/body/eval_jaxpr/psum | solution.py:112
  (110 shorter events, 82.9 us)
Async XLA Ops:
  7.2 10.1 copy-start
  7.2 103.3 %all-reduce.6.cloned.1.call-start = ((), (), s32[]{:S(2)}) async-start(), calls=%async_computation.4 | async-start | bytes 196608 | tf_op jit(solution)/shard_map/psum | solution.py:49
  7.2 5.8 copy-start.1
  14.5 2.7 copy-start.2
  26.9 23.8 %copy-start.4 = (s32[16]{0:T(128)S(1)}, s32[16]{0:T(128)}, u32[]{:S(2)}) copy-start(s32[16]{0:T(128)} %param.19) | copy-start | bytes 196
  50.9 26.9 %copy-start.5 = (s32[16]{0:T(128)}, s32[16]{0:T(128)S(1)}, u32[]{:S(2)}) copy-start(s32[16]{0:T(128)S(1)} %multiply_add_fusion.1) | copy-start | bytes 196
  51.8 13.9 %all-to-all-start.2 = ((s32[16,2,1]{1,2,0:T(1,128)}), s32[16,2,1]{1,2,0:T(1,128)}, u32[]{:S(2)}, u32[]{:S(2)}) async-start(s32[16,2,1]{1,2,0:T(1,128)} %bitcast.4), calls=%async_computation.2 | async-start | bytes 16384 | tf_op jit(solution)/shard_map/all_to_all | solution.py:74
  65.7 12.2 %all-to-all-start.3 = ((s32[16,2,1]{1,2,0:T(1,128)}), s32[16,2,1]{1,2,0:T(1,128)S(1)}, u32[]{:S(2)}, u32[]{:S(2)}) async-start(s32[16,2,1]{1,2,0:T(1,128)} %all-to-all-done.2), calls=%async_computation.3 | async-start | bytes 16384 | tf_op jit(solution)/shard_map/all_to_all | solution.py:73
  113.1 13.1 %all-to-all-start = ((bf16[16,2,192]{2,1,0:T(2,128)(2,1)}), bf16[16,2,192]{2,1,0:T(2,128)(2,1)}, u32[]{:S(2)}, u32[]{:S(2)}) async-start(bf16[16,2,192]{2,1,0:T(2,128)(2,1)} %reshape.84), calls=%async_computation | async-start | bytes 32768 | tf_op jit(solution)/shard_map/all_to_all | solution.py:67
  126.2 11.9 %all-to-all-start.1 = ((bf16[16,2,192]{2,1,0:T(2,128)(2,1)}), bf16[16,2,192]{2,1,0:T(2,128)(2,1)S(1)}, u32[]{:S(2)}, u32[]{:S(2)}) async-start(bf16[16,2,192]{2,1,0:T(2,128)(2,1)} %all-to-all-done), calls=%async_computation.1 | async-start | bytes 32768 | tf_op jit(solution)/shard_map/all_to_all | solution.py:66
  138.8 81.8 %all-reduce.8.cloned.1.call-start = ((), (), s32[]{:S(2)}) async-start(), calls=%async_computation.5 | async-start | bytes 393216 | tf_op jit(solution)/shard_map/while/body/eval_jaxpr/psum | solution.py:12
  220.6 5.8 copy-start.3
  358.2 83.2 %all-reduce.8.cloned.1.call-start = ((), (), s32[]{:S(2)}) async-start(), calls=%async_computation.5 | async-start | bytes 393216 | tf_op jit(solution)/shard_map/while/body/eval_jaxpr/psum | solution.py:12
  441.4 5.8 copy-start.3
  579.0 82.9 %all-reduce.8.cloned.1.call-start = ((), (), s32[]{:S(2)}) async-start(), calls=%async_computation.5 | async-start | bytes 393216 | tf_op jit(solution)/shard_map/while/body/eval_jaxpr/psum | solution.py:12
  661.9 5.8 copy-start.3
  799.5 82.9 %all-reduce.8.cloned.1.call-start = ((), (), s32[]{:S(2)}) async-start(), calls=%async_computation.5 | async-start | bytes 393216 | tf_op jit(solution)/shard_map/while/body/eval_jaxpr/psum | solution.py:12
  882.4 5.8 copy-start.3
Sparse Core Ops, SparseCore 0:
  50.9 59.5 all-reduce.5
  142.8 77.7 all-reduce.7
  362.2 79.1 all-reduce.7
  582.8 79.0 all-reduce.7
  803.2 79.1 all-reduce.7
where the time goes:
time: 1030 us
  blocking collectives  556 us (54%)
  waiting for transfers between devices  330 us (32%)
  matrix products  56.9 us (6%)
  starting transfers between devices  29 us (3%)
  other arithmetic  22 us (2%)
  local copies, waits for them, and re-layouts  15.6 us (2%)
  between operations  13.8 us (1%)
    psum x4, waiting for transfers between devices, spread(): return lax.psum(jnp.where(mine, x, jnp.zeros_like(x)), axis)  278 us
    pmax x4, blocking collectives, score_rows(): largest = lax.pmax(local_max, ('wide', 'narrow'))  265 us
    psum x4, blocking collectives, score_rows(): total, picked = lax.psum((local_total, local_positive), ('wide', 'narrow'))  250 us
    psum x4, blocking collectives, spread(): return lax.psum(jnp.where(mine, x, jnp.zeros_like(x)), axis)  40.4 us
    psum x1, waiting for transfers between devices, local(): pooled = lax.psum(pooled_part, 'narrow') + token_mean  32.4 us
    dot_general x4, matrix products, score_rows(): lax.dot_general(block, slab_old, contract, preferred_element_type=jnp.flo...  23.3 us
    dot_general x1, matrix products, local(): jnp.dot(hidden, down_weight, preferred_element_type=jnp.float32)  22.3 us
  transfers between devices with their start and end apart: 9, of which 9 were waited for; matrix products, arithmetic and copies ran while one was open for 0% of the time, Pallas kernels for 0%

commit v1 on v0

--- a/solution.py
+++ b/solution.py
@@ -109,7 +109,7 @@
         local_total = local_total + jnp.sum(
             jnp.where(valid, jnp.exp(new_scores - largest[:, None]), 0.0), axis=1
         )
-        total, picked = lax.psum((local_total, local_positive), ("wide", "narrow"))
+        total, picked = lax.psum(lax.psum((local_total, local_positive), "wide"), "narrow")
         return largest + jnp.log(total) - picked
 
     def step_body(step, losses):

time: 1030 us -> 969 us (0.941)
  blocking collectives: 556 us -> 498 us
    psum x4 -> x8, blocking collectives: 250 us -> 202 us  [the longest x4 124 us: score_rows(): lax.psum((local_total, local_positive), 'wide')]
where the time goes in v1:
time: 969 us; the launch traced here: 967 us
  blocking collectives  498 us (51%)
  waiting for transfers between devices  329 us (34%)
  matrix products  56.9 us (6%)
  starting transfers between devices  29 us (3%)
  other arithmetic  22 us (2%)
  local copies, waits for them, and re-layouts  15.6 us (2%)
  between operations  13.8 us (1%)
    psum x4, waiting for transfers between devices, spread(): return lax.psum(jnp.where(mine, x, jnp.zeros_like(x)), axis)  276 us
    pmax x4, blocking collectives, score_rows(): largest = lax.pmax(local_max, ('wide', 'narrow'))  265 us
    psum x4, blocking collectives, score_rows(): lax.psum((local_total, local_positive), 'wide')  124 us
    psum x4, blocking collectives, score_rows(): lax.psum(lax.psum((local_total, local_positive), 'wide'), 'narrow')  77.7 us
    psum x1, waiting for transfers between devices, local(): pooled = lax.psum(pooled_part, 'narrow') + token_mean  32.4 us
    psum x4, blocking collectives, spread(): return lax.psum(jnp.where(mine, x, jnp.zeros_like(x)), axis)  30.4 us
    dot_general x4, matrix products, score_rows(): lax.dot_general(block, slab_old, contract, preferred_element_type=jnp.flo...  23.3 us
    dot_general x1, matrix products, local(): jnp.dot(hidden, down_weight, preferred_element_type=jnp.float32)  22.3 us
  transfers between devices with their start and end apart: 9, of which 9 were waited for; matrix products, arithmetic and copies ran while one was open for 0% of the time, Pallas kernels for 0%

profile of v1, /device:TPU:1, one launch (start us, length us, event | category | flops | bytes accessed | tf_op | source)
XLA Modules:
  0.0 967.3 jit_solution(880093934497975516)
XLA Ops:
  17.2 9.7 %fusion.16 = f32[2048,1120]{0,1:T(8,128)} fusion(bf16[2048,1536]{1,0:T(8,128)(2,1)S(1)} %bitcast.50, bf16[1536,1120]{0,1:T(8,128)(2,1)S(1)} %copy-done), kind=kOutput, calls=%fused_computation.49 | convolution fusion | flops 7046430720 | bytes 18907136 | tf_op jit(solution)/shard_map/dot_general | solution.py:42
  26.9 22.3 %bitcast_reduce_fusion = f32[16,1536]{1,0:T(8,128)} fusion(bf16[1120,1536]{1,0:T(8,128)(2,1)} %param.17, bf16[2048,1536]{1,0:T(8,128)(2,1)} %bitcast.51, bf16[1536,1120]{0,1:T(8,128)(2,1)} %param.16, f32[2048,1120]{0,1:T(8,128)} %fusion.16), kind=kOutput, calls=%fused_computation.19 | convolution fusion | flops 14109745152 | bytes 22446080 | tf_op jit(solution)/shard_map/dot_general | solution.py:45
  51.8 7.6 all-to-all-start.2
  65.7 7.6 all-to-all-start.3
  78.1 32.4 %all-reduce.9.cloned.1.call-done = f32[16,1536]{1,0:T(8,128)} async-done(((f32[16,1536]{1,0:T(8,128)}), f32[16,1536]{1,0:T(8,128)}) %all-reduce.9.cloned.1.call-update) | async-done | bytes 98320 | tf_op jit(solution)/shard_map/psum | solution.py:49
  138.8 822.0 %while.14 = (s32[]{:T(128)}, f32[4,64]{1,0:T(4,128)}, s32[4]{0:T(128)}, bf16[1,64,1536]{2,1,0:T(8,128)(2,1)}, bf16[2048,1536]{1,0:T(8,128)(2,1)}, /*index=5*/pre...) while((s32[]{:T(128)}, f32[4,64]{1,0:T(4,128)}, ...), condition=%wide.region_21.22_spmd.clone, body=%wide.region_7.21_spmd.clone.sunk | while | flops 404558720 | bytes 10133544 | solution.py:122
  141.6 9.3 psum.83
  150.9 69.7 %all-reduce.11.cloned.1.call-done = bf16[64,1536]{1,0:T(8,128)(2,1)} async-done(((bf16[64,1536]{1,0:T(8,128)(2,1)}), bf16[64,1536]{1,0:T(8,128)(2,1)}) %all-reduce.11.cloned.1.call-update) | async-done | bytes 196624 | tf_op jit(solution)/shard_map/while/body/eval_jaxpr/psum | solution.py:12
  226.6 66.3 %pmax.13 = f32[64]{0:T(128)S(1)} all-reduce(f32[64]{0:T(128)S(1)} %max.11), channel_id=1, replica_groups=mesh['wide'=16,'narrow'=8] {'wide','narrow'}, use_global_device_ids=true, to_apply=%region_11.11 | all-reduce | flops 64 | bytes 512 | tf_op jit(solution)/shard_map/while/body/eval_jaxpr/pmax | solution.py:107
  294.4 31.1 %all-reduce.4 = (f32[64]{0:T(128)S(1)}, f32[64]{0:T(128)S(1)}) all-reduce(f32[64]{0:T(128)S(1)} %add.191, f32[64]{0:T(128)S(1)} %add.192), channel_id=1, replica_groups=mesh['wide'=16,'narrow'=8] {'wide'}, use_global_device_ids=true, to_apply=%region_19.19 | all-reduce | flops 128 | bytes 1024 | tf_op jit(solution)/shard_map/while/body/eval_jaxpr/psum | solution.py:112
  325.5 19.4 %all-reduce.5 = (f32[64]{0:T(128)S(1)}, f32[64]{0:T(128)S(1)}) all-reduce(f32[64]{0:T(128)S(1)} %get-tuple-element.312, f32[64]{0:T(128)S(1)} %get-tuple-element.313), channel_id=1, replica_groups=mesh['wide'=16,'narrow'=8] {'narrow'}, use_global_device_ids=true, to_apply=%region_20.20 | all-reduce | flops 128 | bytes 1024 | tf_op jit(solution)/shard_map/while/body/eval_jaxpr/psum | solution.py:112
  355.9 69.7 %all-reduce.11.cloned.1.call-done = bf16[64,1536]{1,0:T(8,128)(2,1)} async-done(((bf16[64,1536]{1,0:T(8,128)(2,1)}), bf16[64,1536]{1,0:T(8,128)(2,1)}) %all-reduce.11.cloned.1.call-update) | async-done | bytes 196624 | tf_op jit(solution)/shard_map/while/body/eval_jaxpr/psum | solution.py:12
  431.6 66.3 %pmax.13 = f32[64]{0:T(128)S(1)} all-reduce(f32[64]{0:T(128)S(1)} %max.11), channel_id=1, replica_groups=mesh['wide'=16,'narrow'=8] {'wide','narrow'}, use_global_device_ids=true, to_apply=%region_11.11 | all-reduce | flops 64 | bytes 512 | tf_op jit(solution)/shard_map/while/body/eval_jaxpr/pmax | solution.py:107
  499.4 31.1 %all-reduce.4 = (f32[64]{0:T(128)S(1)}, f32[64]{0:T(128)S(1)}) all-reduce(f32[64]{0:T(128)S(1)} %add.191, f32[64]{0:T(128)S(1)} %add.192), channel_id=1, replica_groups=mesh['wide'=16,'narrow'=8] {'wide'}, use_global_device_ids=true, to_apply=%region_19.19 | all-reduce | flops 128 | bytes 1024 | tf_op jit(solution)/shard_map/while/body/eval_jaxpr/psum | solution.py:112
  530.5 19.4 %all-reduce.5 = (f32[64]{0:T(128)S(1)}, f32[64]{0:T(128)S(1)}) all-reduce(f32[64]{0:T(128)S(1)} %get-tuple-element.312, f32[64]{0:T(128)S(1)} %get-tuple-element.313), channel_id=1, replica_groups=mesh['wide'=16,'narrow'=8] {'narrow'}, use_global_device_ids=true, to_apply=%region_20.20 | all-reduce | flops 128 | bytes 1024 | tf_op jit(solution)/shard_map/while/body/eval_jaxpr/psum | solution.py:112
  561.0 69.5 %all-reduce.11.cloned.1.call-done = bf16[64,1536]{1,0:T(8,128)(2,1)} async-done(((bf16[64,1536]{1,0:T(8,128)(2,1)}), bf16[64,1536]{1,0:T(8,128)(2,1)}) %all-reduce.11.cloned.1.call-update) | async-done | bytes 196624 | tf_op jit(solution)/shard_map/while/body/eval_jaxpr/psum | solution.py:12
  636.5 66.3 %pmax.13 = f32[64]{0:T(128)S(1)} all-reduce(f32[64]{0:T(128)S(1)} %max.11), channel_id=1, replica_groups=mesh['wide'=16,'narrow'=8] {'wide','narrow'}, use_global_device_ids=true, to_apply=%region_11.11 | all-reduce | flops 64 | bytes 512 | tf_op jit(solution)/shard_map/while/body/eval_jaxpr/pmax | solution.py:107
  704.2 31.1 %all-reduce.4 = (f32[64]{0:T(128)S(1)}, f32[64]{0:T(128)S(1)}) all-reduce(f32[64]{0:T(128)S(1)} %add.191, f32[64]{0:T(128)S(1)} %add.192), channel_id=1, replica_groups=mesh['wide'=16,'narrow'=8] {'wide'}, use_global_device_ids=true, to_apply=%region_19.19 | all-reduce | flops 128 | bytes 1024 | tf_op jit(solution)/shard_map/while/body/eval_jaxpr/psum | solution.py:112
  735.3 19.4 %all-reduce.5 = (f32[64]{0:T(128)S(1)}, f32[64]{0:T(128)S(1)}) all-reduce(f32[64]{0:T(128)S(1)} %get-tuple-element.312, f32[64]{0:T(128)S(1)} %get-tuple-element.313), channel_id=1, replica_groups=mesh['wide'=16,'narrow'=8] {'narrow'}, use_global_device_ids=true, to_apply=%region_20.20 | all-reduce | flops 128 | bytes 1024 | tf_op jit(solution)/shard_map/while/body/eval_jaxpr/psum | solution.py:112
  758.8 8.8 psum.83
  767.6 67.5 %all-reduce.11.cloned.1.call-done = bf16[64,1536]{1,0:T(8,128)(2,1)} async-done(((bf16[64,1536]{1,0:T(8,128)(2,1)}), bf16[64,1536]{1,0:T(8,128)(2,1)}) %all-reduce.11.cloned.1.call-update) | async-done | bytes 196624 | tf_op jit(solution)/shard_map/while/body/eval_jaxpr/psum | solution.py:12
  841.2 66.3 %pmax.13 = f32[64]{0:T(128)S(1)} all-reduce(f32[64]{0:T(128)S(1)} %max.11), channel_id=1, replica_groups=mesh['wide'=16,'narrow'=8] {'wide','narrow'}, use_global_device_ids=true, to_apply=%region_11.11 | all-reduce | flops 64 | bytes 512 | tf_op jit(solution)/shard_map/while/body/eval_jaxpr/pmax | solution.py:107
  909.0 31.1 %all-reduce.4 = (f32[64]{0:T(128)S(1)}, f32[64]{0:T(128)S(1)}) all-reduce(f32[64]{0:T(128)S(1)} %add.191, f32[64]{0:T(128)S(1)} %add.192), channel_id=1, replica_groups=mesh['wide'=16,'narrow'=8] {'wide'}, use_global_device_ids=true, to_apply=%region_19.19 | all-reduce | flops 128 | bytes 1024 | tf_op jit(solution)/shard_map/while/body/eval_jaxpr/psum | solution.py:112
  940.1 19.4 %all-reduce.5 = (f32[64]{0:T(128)S(1)}, f32[64]{0:T(128)S(1)}) all-reduce(f32[64]{0:T(128)S(1)} %get-tuple-element.312, f32[64]{0:T(128)S(1)} %get-tuple-element.313), channel_id=1, replica_groups=mesh['wide'=16,'narrow'=8] {'narrow'}, use_global_device_ids=true, to_apply=%region_20.20 | all-reduce | flops 128 | bytes 1024 | tf_op jit(solution)/shard_map/while/body/eval_jaxpr/psum | solution.py:112
  (114 shorter events, 109.0 us)
Async XLA Ops:
  7.2 10.1 %copy-start = (bf16[1536,1120]{0,1:T(8,128)(2,1)S(1)}, bf16[1536,1120]{0,1:T(8,128)(2,1)}, u32[]{:S(2)}) copy-start(bf16[1536,1120]{0,1:T(8,128)(2,1)} %param.15) | copy-start | bytes 10321924
  7.2 103.3 %all-reduce.9.cloned.1.call-start = ((), (), s32[]{:S(2)}) async-start(), calls=%async_computation.4 | async-start | bytes 196608 | tf_op jit(solution)/shard_map/psum | solution.py:49
  7.2 5.8 copy-start.1
  14.5 2.7 copy-start.2
  26.9 23.8 %copy-start.4 = (s32[16]{0:T(128)S(1)}, s32[16]{0:T(128)}, u32[]{:S(2)}) copy-start(s32[16]{0:T(128)} %param.19) | copy-start | bytes 196
  50.9 26.9 %copy-start.5 = (s32[16]{0:T(128)}, s32[16]{0:T(128)S(1)}, u32[]{:S(2)}) copy-start(s32[16]{0:T(128)S(1)} %multiply_add_fusion.1) | copy-start | bytes 196
  51.8 13.9 %all-to-all-start.2 = ((s32[16,2,1]{1,2,0:T(1,128)}), s32[16,2,1]{1,2,0:T(1,128)}, u32[]{:S(2)}, u32[]{:S(2)}) async-start(s32[16,2,1]{1,2,0:T(1,128)} %bitcast.4), calls=%async_computation.2 | async-start | bytes 16384 | tf_op jit(solution)/shard_map/all_to_all | solution.py:74
  65.7 12.2 %all-to-all-start.3 = ((s32[16,2,1]{1,2,0:T(1,128)}), s32[16,2,1]{1,2,0:T(1,128)S(1)}, u32[]{:S(2)}, u32[]{:S(2)}) async-start(s32[16,2,1]{1,2,0:T(1,128)} %all-to-all-done.2), calls=%async_computation.3 | async-start | bytes 16384 | tf_op jit(solution)/shard_map/all_to_all | solution.py:73
  113.1 13.1 %all-to-all-start = ((bf16[16,2,192]{2,1,0:T(2,128)(2,1)}), bf16[16,2,192]{2,1,0:T(2,128)(2,1)}, u32[]{:S(2)}, u32[]{:S(2)}) async-start(bf16[16,2,192]{2,1,0:T(2,128)(2,1)} %reshape.84), calls=%async_computation | async-start | bytes 32768 | tf_op jit(solution)/shard_map/all_to_all | solution.py:67
  126.2 11.9 %all-to-all-start.1 = ((bf16[16,2,192]{2,1,0:T(2,128)(2,1)}), bf16[16,2,192]{2,1,0:T(2,128)(2,1)S(1)}, u32[]{:S(2)}, u32[]{:S(2)}) async-start(bf16[16,2,192]{2,1,0:T(2,128)(2,1)} %all-to-all-done), calls=%async_computation.1 | async-start | bytes 32768 | tf_op jit(solution)/shard_map/all_to_all | solution.py:66
  138.8 81.8 %all-reduce.11.cloned.1.call-start = ((), (), s32[]{:S(2)}) async-start(), calls=%async_computation.5 | async-start | bytes 393216 | tf_op jit(solution)/shard_map/while/body/eval_jaxpr/psum | solution.py:12
  220.6 5.8 copy-start.3
  346.2 79.4 %all-reduce.11.cloned.1.call-start = ((), (), s32[]{:S(2)}) async-start(), calls=%async_computation.5 | async-start | bytes 393216 | tf_op jit(solution)/shard_map/while/body/eval_jaxpr/psum | solution.py:12
  425.6 5.8 copy-start.3
  551.2 79.2 %all-reduce.11.cloned.1.call-start = ((), (), s32[]{:S(2)}) async-start(), calls=%async_computation.5 | async-start | bytes 393216 | tf_op jit(solution)/shard_map/while/body/eval_jaxpr/psum | solution.py:12
  630.4 5.8 copy-start.3
  756.1 79.1 %all-reduce.11.cloned.1.call-start = ((), (), s32[]{:S(2)}) async-start(), calls=%async_computation.5 | async-start | bytes 393216 | tf_op jit(solution)/shard_map/while/body/eval_jaxpr/psum | solution.py:12
  835.2 5.8 copy-start.3
Sparse Core Ops, SparseCore 0:
  50.9 59.5 all-reduce.8
  142.8 77.7 all-reduce.10
  350.2 75.3 all-reduce.10
  555.0 75.3 all-reduce.10
  759.7 75.3 all-reduce.10
